TPU v7x, 256 devices: a whole 4x4x8 slice. The times are simulated.
256 devices in a mesh: tm: 8 (over y, core), space: 32 (over x, z).
Axes of the slice: x: 4, y: 4, z: 8, core: 2. Of those that a mesh axis runs over, the one named last changes fastest.
Arguments:
- snapshots: float32 [2048, 128, 1024], P('space', None, 'tm'), may hold values from -6 to 6
- land_mask: int32 [2048, 128], P('space'), may hold values 0 or 1
- taps_rows: float32 [6], replicated, may hold values from -2.5 to 2.5
- taps_cols: float32 [6], replicated, may hold values from -2.5 to 2.5
- probes: float32 [1024, 64, 128], P('space'), may hold values from -6 to 6
Outputs:
- basis: float32 [1024, 64, 128], P('space', None, 'tm')
- coefficients: float32 [128, 128], P('tm')
All inputs are finite; a program needn't handle non-finite values. No bound on the sum of `land_mask` on one device may be relied on, other than what follows from the above.
Results may differ from a plain program's by a relative error of at most 0.00028.
Values sent between devices are 32-bit elements; how exact they have to be, the bound alone decides.
A program may use at most 64 MiB of HBM per device.

v0:
```python
import jax
import jax.numpy as jnp
from jax import lax
from jax.sharding import PartitionSpec as P

SIGN_STEPS = 8
exact_dot = lax.Precision.HIGHEST


def padded_2(x, sides, width):
    for axis, dim in sides:
        size, length = (lax.axis_size(axis), x.shape[dim])
        up = [(i, (i + 1) % size) for i in range(size - 1)]
        down = [(j, i) for i, j in up]
        last = lax.slice_in_dim(x, length - width, length, axis=dim)
        initial = lax.slice_in_dim(x, 0, width, axis=dim)
        before = lax.ppermute(last, axis, up)
        after = lax.ppermute(initial, axis, down)
        x = jnp.concatenate([before, x, after], axis=dim)
    return x


def partner(block, axis, distance):
    count = lax.axis_size(axis)
    route = []
    for low in range(count):
        high = low | 1 << distance
        if high != low and high < count:
            route += [(low, high), (high, low)]
    return lax.ppermute(block, axis, route)


def band_matrix(tap_values, out_count, in_width, shift_by):
    row_ids = lax.broadcasted_iota(jnp.int32, (out_count, in_width), 0)
    col_ids = lax.broadcasted_iota(jnp.int32, (out_count, in_width), 1)
    tap_offset = col_ids - 2 * row_ids - shift_by
    band_table = jnp.zeros((out_count, in_width), jnp.float32)
    for tap_index in range(6):
        band_table = band_table + jnp.where(tap_offset == tap_index, tap_values[tap_index], 0.0)
    return band_table


def merge_level(paired):
    partial_gram = jnp.einsum("gra,grb->gab", paired, paired, precision=exact_dot)
    gram_total = lax.psum(partial_gram, "space")
    order_size = gram_total.shape[-1]
    identity = jnp.eye(order_size, dtype=jnp.float32)
    mean_eig = jnp.sum(gram_total * identity, axis=(1, 2)) / order_size
    shifted = gram_total - mean_eig[:, None, None] * identity
    norm_scale = jnp.sqrt(jnp.sum(shifted * shifted, axis=(1, 2)) + 1e-06)
    sign_iter = shifted / norm_scale[:, None, None]
    for sweep_index in range(SIGN_STEPS):
        square = jnp.einsum("gab,gbc->gac", sign_iter, sign_iter, precision=exact_dot)
        sign_iter = 1.5 * sign_iter - 0.5 * jnp.einsum(
            "gab,gbc->gac", sign_iter, square, precision=exact_dot
        )
    projector = 0.5 * (identity + sign_iter)
    half_order = order_size // 2
    combine = projector[:, :, :half_order] + projector[:, :, half_order:]
    return jnp.einsum("gra,gab->grb", paired, combine, precision=exact_dot)


def local(snapshots, land_mask, taps_rows, taps_cols, probes):
    rows_dev, cell_cols, columns = snapshots.shape
    ocean_field = snapshots * land_mask.astype(jnp.float32)[:, :, None]
    across = band_matrix(taps_cols, cell_cols // 2, cell_cols, -2)
    narrowed = jnp.einsum("jy,xys->xjs", across, ocean_field, precision=exact_dot)
    padded = padded_2(narrowed, (("space", 0),), 3)
    row_filter = band_matrix(taps_rows, rows_dev // 2, rows_dev + 6, 1)
    filtered = jnp.einsum("ip,pjs->ijs", row_filter, padded, precision=exact_dot)
    cell_rows = rows_dev // 2 * (cell_cols // 2)
    factor = filtered.reshape(cell_rows, columns)
    flat_probes = probes.reshape(cell_rows, probes.shape[2])
    levels = lax.axis_size("tm").bit_length() - 1
    position = lax.axis_index("tm")
    merged = factor
    for level_index in range(levels):
        partner_fac = partner(merged, "tm", level_index)
        is_upper = position >> level_index & 1 == 1
        lower_part = jnp.where(is_upper, partner_fac, merged)
        upper_part = jnp.where(is_upper, merged, partner_fac)
        merged = merge_level(jnp.concatenate([lower_part, upper_part], axis=1)[None])[0]
    width_dev = columns // lax.axis_size("tm")
    col_start = position * width_dev
    partial_coef = jnp.einsum("rs,rp->sp", merged, flat_probes, precision=exact_dot)
    coefficients = lax.psum(partial_coef, "space")
    basis_own = lax.dynamic_slice_in_dim(merged, col_start, width_dev, 1)
    coef_own = lax.dynamic_slice_in_dim(coefficients, col_start, width_dev, 0)
    return (basis_own.reshape(rows_dev // 2, cell_cols // 2, width_dev), coef_own)


def solution(mesh):
    placed = (P("space", None, "tm"), P("space", None), P(), P(), P("space", None, None))
    return jax.shard_map(
        local,
        mesh=mesh,
        in_specs=placed,
        out_specs=(P("space", None, "tm"), P("tm", None)),
        check_vma=False,
    )
```

profile of v0, /device:TPU:2, one launch (start us, length us, event | category | flops | bytes accessed | tf_op | source)
XLA Modules:
  0.0 723.5 jit_solution(15306966266729676532)
XLA Ops:
  9.5 9.0 %fusion.11 = f32[64,64,128]{2,1,0:T(8,128)S(1)} fusion(f32[64,128,128]{2,1,0:T(8,128)} %param.5, f32[64,128]{1,0:T(8,128)S(1)} %convert_element_type.22, f32[]{:T(128)} %bitcast.12, f32[]{:T(128)} %bitcast.11, f32[]{:T(128)} %bitcast.10, f32[]{:T(128)} %bitcast.9, f32[]{:T(128)} %bitcast.8, f32[]{:T(128)} %bitcast.7, s32[64]{0:T(128)S(1)} %iota_multiply_fusion), kind=kOutput, calls=%fused_computation.15 | convolution fusion | flops 806510592 | bytes 6324504 | tf_op jit(solution)/shard_map/jy,xys->xjs/dot_general | solution.py:67
  18.6 3.8 collective-permute-start
  22.4 5.8 collective-permute-start.1
  30.8 6.5 fusion.2
  38.9 1.9 collective-permute-done.2
  40.7 1.7 broadcast_select_fusion.1
  42.4 4.2 fusion.14
  47.1 145.3 %all-reduce.5.cloned.1.call-done = f32[1,256,256]{2,1,0:T(8,128)} async-done(((f32[1,256,256]{2,1,0:T(8,128)}), f32[1,256,256]{2,1,0:T(8,128)}) %all-reduce.5.cloned.1.call-update) | async-done | bytes 262160 | tf_op jit(solution)/shard_map/psum | solution.py:45
  194.6 1.6 multiply_reduce_fusion.2
  205.3 3.3 fusion.9
  210.1 19.3 %collective-permute-done.3 = f32[2048,128]{0,1:T(8,128)} collective-permute-done((f32[2048,128]{0,1:T(8,128)}, f32[2048,128]{0,1:T(8,128)}, u32[]{:S(2)}, u32[]{:S(2)}) %collective-permute-start.3) | collective-permute-done | bytes 1048608 | tf_op jit(solution)/shard_map/ppermute | solution.py:30
  229.4 1.7 broadcast_select_fusion.3
  231.1 2.6 fusion.15
  233.9 141.9 %all-reduce.7.cloned.1.call-done = f32[1,256,256]{2,1,0:T(8,128)} async-done(((f32[1,256,256]{2,1,0:T(8,128)}), f32[1,256,256]{2,1,0:T(8,128)}) %all-reduce.7.cloned.1.call-update) | async-done | bytes 262160 | tf_op jit(solution)/shard_map/psum | solution.py:45
  378.0 1.6 multiply_reduce_fusion.1
  388.7 2.3 fusion.7
  391.0 3.0 collective-permute-start.4
  394.0 19.3 %collective-permute-done.4 = f32[2048,128]{0,1:T(8,128)} collective-permute-done((f32[2048,128]{0,1:T(8,128)}, f32[2048,128]{0,1:T(8,128)}, u32[]{:S(2)}, u32[]{:S(2)}) %collective-permute-start.4) | collective-permute-done | bytes 1048608 | tf_op jit(solution)/shard_map/ppermute | solution.py:30
  413.3 1.7 broadcast_select_fusion.5
  415.0 2.6 fusion.16
  417.9 141.8 %all-reduce.9.cloned.1.call-done = f32[1,256,256]{2,1,0:T(8,128)} async-done(((f32[1,256,256]{2,1,0:T(8,128)}), f32[1,256,256]{2,1,0:T(8,128)}) %all-reduce.9.cloned.1.call-update) | async-done | bytes 262160 | tf_op jit(solution)/shard_map/psum | solution.py:45
  562.0 1.6 multiply_reduce_fusion
  574.0 1.8 fusion.268
  576.8 138.7 %all-reduce.11.cloned.1.call-done = f32[128,128]{1,0:T(8,128)} async-done(((f32[128,128]{1,0:T(8,128)}), f32[128,128]{1,0:T(8,128)}) %all-reduce.11.cloned.1.call-update) | async-done | bytes 65552 | tf_op jit(solution)/shard_map/psum | solution.py:86
  (86 shorter events, 42.0 us)
Async XLA Ops:
  7.2 566.8 %copy-start = (f32[32,64,128]{2,1,0:T(8,128)S(1)}, f32[32,64,128]{2,1,0:T(8,128)}, u32[]{:S(2)}) copy-start(f32[32,64,128]{2,1,0:T(8,128)} %param.9) | copy-start | bytes 3145732
  7.2 185.2 %all-reduce.5.cloned.1.call-start = ((), (), s32[]{:S(2)}) async-start(), calls=%async_computation | async-start | bytes 524288 | tf_op jit(solution)/shard_map/psum | solution.py:45
  9.5 18.7 %copy-start.4 = (f32[6]{0:T(128)S(1)}, f32[6]{0:T(128)}, u32[]{:S(2)}) copy-start(f32[6]{0:T(128)} %param.7) | copy-start | bytes 76
  18.6 10.5 %collective-permute-start = (f32[3,64,128]{2,1,0:T(8,128)S(1)}, f32[3,64,128]{2,1,0:T(8,128)S(1)}, u32[]{:S(2)}, u32[]{:S(2)}) collective-permute-start(f32[3,64,128]{2,1,0:T(8,128)S(1)} %get-tuple-element.10), channel_id=1, source_target_pairs={{0,1},{1,2},{2,3},{3,4},{4,5},{5,6},{6,7},{7,8},{8,9},{9,10},{10,1... | collective-permute-start | bytes 294920 | tf_op jit(solution)/shard_map/ppermute | solution.py:17
  22.4 8.0 %collective-permute-start.1 = (f32[3,64,128]{2,1,0:T(8,128)S(1)}, f32[3,64,128]{2,1,0:T(8,128)S(1)}, u32[]{:S(2)}, u32[]{:S(2)}) collective-permute-start(f32[3,64,128]{2,1,0:T(8,128)S(1)} %get-tuple-element.11), channel_id=1, source_target_pairs={{1,0},{2,1},{3,2},{4,3},{5,4},{6,5},{7,6},{8,7},{9,8},{10,9},{11,1... | collective-permute-start | bytes 294920 | tf_op jit(solution)/shard_map/ppermute | solution.py:18
  37.8 1.0 copy-start.3
  37.9 2.9 collective-permute-start.2
  46.6 329.2 %all-reduce.7.cloned.1.call-start = ((), (), s32[]{:S(2)}) async-start(), calls=%async_computation.1 | async-start | bytes 524288 | tf_op jit(solution)/shard_map/psum | solution.py:45
  208.6 20.8 %collective-permute-start.3 = (f32[2048,128]{0,1:T(8,128)}, f32[2048,128]{0,1:T(8,128)}, u32[]{:S(2)}, u32[]{:S(2)}) collective-permute-start(f32[2048,128]{0,1:T(8,128)} %fusion.9), channel_id=1, source_target_pairs={{0,64},{64,0},{32,96},{96,32},{128,192},{192,128},{160,224},{224,1... | collective-permute-start | bytes 3145736 | tf_op jit(solution)/shard_map/ppermute | solution.py:30
  233.7 326.0 %all-reduce.9.cloned.1.call-start = ((), (), s32[]{:S(2)}) async-start(), calls=%async_computation.2 | async-start | bytes 524288 | tf_op jit(solution)/shard_map/psum | solution.py:45
  391.0 22.3 %collective-permute-start.4 = (f32[2048,128]{0,1:T(8,128)}, f32[2048,128]{0,1:T(8,128)}, u32[]{:S(2)}, u32[]{:S(2)}) collective-permute-start(f32[2048,128]{0,1:T(8,128)} %fusion.7), channel_id=1, source_target_pairs={{0,128},{128,0},{32,160},{160,32},{64,192},{192,64},{96,224},{224,... | collective-permute-start | bytes 3145736 | tf_op jit(solution)/shard_map/ppermute | solution.py:30
  415.0 150.7 %copy-start.1 = (f32[2048,128]{0,1:T(8,128)}, f32[2048,128]{0,1:T(8,128)S(1)}, u32[]{:S(2)}) copy-start(f32[2048,128]{0,1:T(8,128)S(1)} %get-tuple-element.5) | copy-start | bytes 3145732
  417.6 297.8 %all-reduce.11.cloned.1.call-start = ((), (), s32[]{:S(2)}) async-start(), calls=%async_computation.3 | async-start | bytes 131072 | tf_op jit(solution)/shard_map/psum | solution.py:86
  570.3 2.4 copy-start.2
Sparse Core Ops, SparseCore 0:
  46.7 145.6 all-reduce.4
  233.8 141.9 all-reduce.6
  417.7 141.9 all-reduce.8
  575.9 139.4 all-reduce.10
where the time goes:
time: 731 us; the launch traced here: 724 us
  waiting for transfers between devices  610 us (83%)
  matrix products  58.2 us (8%)
  between operations  18.6 us (3%)
  other arithmetic  15.7 us (2%)
  starting transfers between devices  15.3 us (2%)
    psum x3, waiting for transfers between devices, merge_level(): gram_total = lax.psum(partial_gram, 'space')  429 us
    psum x1, waiting for transfers between devices, local(): coefficients = lax.psum(partial_coef, 'space')  139 us
    ppermute x3, waiting for transfers between devices, partner(): return lax.ppermute(block, axis, route)  40.4 us
  transfers between devices with their start and end apart: 9, of which 9 were waited for; matrix products, arithmetic and copies ran while one was open for 0% of the time, Pallas kernels for 0%

commit v1 on v0

--- a/solution.py
+++ b/solution.py
@@ -42,7 +42,8 @@
 
 def merge_level(paired):
     partial_gram = jnp.einsum("gra,grb->gab", paired, paired, precision=exact_dot)
-    gram_total = lax.psum(partial_gram, "space")
+    parts = lax.all_gather(partial_gram, "space")
+    gram_total = jnp.sum(parts, axis=0)
     order_size = gram_total.shape[-1]
     identity = jnp.eye(order_size, dtype=jnp.float32)
     mean_eig = jnp.sum(gram_total * identity, axis=(1, 2)) / order_size

time: 731 us -> 597 us (0.82)
  waiting for transfers between devices: 610 us -> 475 us
    psum x3 -> x0, waiting for transfers between devices: 429 us -> none  [merge_level(): gram_total = lax.psum(partial_gram, 'space')]
    all_gather x0 -> x3, waiting for transfers between devices: none -> 287 us  [merge_level(): parts = lax.all_gather(partial_gram, 'space')]
    reduce_sum x0 -> x3, other arithmetic: none -> 11.8 us  [merge_level(): gram_total = jnp.sum(parts, axis=0)]
    ppermute x3, waiting for transfers between devices: 40.4 us -> 47.7 us  [partner(): return lax.ppermute(block, axis, route)]
where the time goes in v1:
time: 597 us; the launch traced here: 590 us
  waiting for transfers between devices  475 us (80%)
  matrix products  52 us (9%)
  other arithmetic  21.5 us (4%)
  between operations  18.6 us (3%)
  starting transfers between devices  15.3 us (3%)
  local copies, waits for them, and re-layouts  7.12 us (1%)
    all_gather x3, waiting for transfers between devices, merge_level(): parts = lax.all_gather(partial_gram, 'space')  287 us
    psum x1, waiting for transfers between devices, local(): coefficients = lax.psum(partial_coef, 'space')  139 us
    ppermute x3, waiting for transfers between devices, partner(): return lax.ppermute(block, axis, route)  47.7 us
  transfers between devices with their start and end apart: 9, of which 9 were waited for; matrix products, arithmetic and copies ran while one was open for 0% of the time, Pallas kernels for 0%

profile of v1, /device:TPU:2, one launch (start us, length us, event | category | flops | bytes accessed | tf_op | source)
XLA Modules:
  0.0 589.6 jit_solution(4095015698481230483)
XLA Ops:
  7.2 1.5 fusion.198
  9.5 9.0 %fusion.11 = f32[64,64,128]{2,1,0:T(8,128)S(1)} fusion(f32[64,128,128]{2,1,0:T(8,128)} %param.5, f32[64,128]{1,0:T(8,128)S(1)} %convert_element_type.45, f32[]{:T(128)} %bitcast.12, f32[]{:T(128)} %bitcast.11, f32[]{:T(128)} %bitcast.10, f32[]{:T(128)} %bitcast.9, f32[]{:T(128)} %bitcast.8, f32[]{:T(128)} %bitcast.7, s32[64]{0:T(128)S(1)} %iota_multiply_fusion), kind=kOutput, calls=%fused_computation.15 | convolution fusion | flops 806510592 | bytes 6324504 | tf_op jit(solution)/shard_map/jy,xys->xjs/dot_general | solution.py:68
  18.6 3.8 collective-permute-start
  22.4 5.8 collective-permute-start.1
  30.8 6.5 %fusion.2 = f32[32,64,128]{2,0,1:T(8,128)S(1)} fusion(f32[70,64,128]{2,1,0:T(8,128)S(1)} %pad_maximum_fusion, f32[]{:T(128)} %bitcast.5, f32[]{:T(128)} %bitcast.4, f32[]{:T(128)} %bitcast.3, f32[]{:T(128)} %bitcast.2, f32[]{:T(128)} %bitcast.1, f32[]{:T(128)} %bitcast, s32[32]{0:T(128)S(1)} %iota_multiply_fusion.1), kind=kOutput, calls=%fused_computation.2 | convolution fusion | flops 220243520 | bytes 3342488 | tf_op jit(solution)/shard_map/ip,pjs->ijs/dot_general | solution.py:71
  38.9 1.9 collective-permute-done.2
  40.7 1.7 broadcast_select_fusion.1
  42.4 4.2 fusion.10
  47.1 97.5 %all-gather.7.cloned.1.call-done = f32[8192,256]{1,0:T(8,128)} async-done(((f32[256,256]{1,0:T(8,128)}), f32[8192,256]{1,0:T(8,128)}) %all-gather.7.cloned.1.call-update) | async-done | bytes 8388624 | tf_op jit(solution)/shard_map/all_gather | solution.py:45
  144.6 3.9 reduce.9
  157.5 3.3 fusion.9
  162.3 23.0 %collective-permute-done.3 = f32[2048,128]{0,1:T(8,128)} collective-permute-done((f32[2048,128]{0,1:T(8,128)}, f32[2048,128]{0,1:T(8,128)}, u32[]{:S(2)}, u32[]{:S(2)}) %collective-permute-start.3) | collective-permute-done | bytes 1048608 | tf_op jit(solution)/shard_map/ppermute | solution.py:30
  185.3 1.7 broadcast_select_fusion.3
  187.0 2.6 fusion.8
  189.8 94.8 %all-gather.9.cloned.1.call-done = f32[8192,256]{1,0:T(8,128)} async-done(((f32[256,256]{1,0:T(8,128)}), f32[8192,256]{1,0:T(8,128)}) %all-gather.9.cloned.1.call-update) | async-done | bytes 8388624 | tf_op jit(solution)/shard_map/all_gather | solution.py:45
  284.6 3.9 reduce.10
  297.4 2.3 fusion.7
  299.8 3.0 collective-permute-start.4
  302.8 22.9 %collective-permute-done.4 = f32[2048,128]{0,1:T(8,128)S(1)} collective-permute-done((f32[2048,128]{0,1:T(8,128)}, f32[2048,128]{0,1:T(8,128)S(1)}, u32[]{:S(2)}, u32[]{:S(2)}) %collective-permute-start.4) | collective-permute-done | bytes 1048608 | tf_op jit(solution)/shard_map/ppermute | solution.py:30
  328.1 2.6 fusion.6
  331.0 94.8 %all-gather.11.cloned.1.call-done = f32[8192,256]{1,0:T(8,128)} async-done(((f32[256,256]{1,0:T(8,128)}), f32[8192,256]{1,0:T(8,128)}) %all-gather.11.cloned.1.call-update) | async-done | bytes 8388624 | tf_op jit(solution)/shard_map/all_gather | solution.py:45
  425.8 3.9 reduce.11
  440.0 1.8 fusion.220
  442.8 138.8 %all-reduce.2.cloned.1.call-done = f32[128,128]{1,0:T(8,128)} async-done(((f32[128,128]{1,0:T(8,128)}), f32[128,128]{1,0:T(8,128)}) %all-reduce.2.cloned.1.call-update) | async-done | bytes 65552 | tf_op jit(solution)/shard_map/psum | solution.py:87
  (89 shorter events, 35.8 us)
Async XLA Ops:
  7.2 432.8 %copy-start = (f32[32,64,128]{2,1,0:T(8,128)S(1)}, f32[32,64,128]{2,1,0:T(8,128)}, u32[]{:S(2)}) copy-start(f32[32,64,128]{2,1,0:T(8,128)} %param.9) | copy-start | bytes 3145732
  7.2 137.5 %all-gather.7.cloned.1.call-start = ((), (), s32[]{:S(2)}) async-start(), calls=%async_computation.1 | async-start | bytes 8650752 | tf_op jit(solution)/shard_map/all_gather | solution.py:45
  9.5 18.7 %copy-start.4 = (f32[6]{0:T(128)S(1)}, f32[6]{0:T(128)}, u32[]{:S(2)}) copy-start(f32[6]{0:T(128)} %param.7) | copy-start | bytes 76
  18.6 10.5 %collective-permute-start = (f32[3,64,128]{2,1,0:T(8,128)S(1)}, f32[3,64,128]{2,1,0:T(8,128)S(1)}, u32[]{:S(2)}, u32[]{:S(2)}) collective-permute-start(f32[3,64,128]{2,1,0:T(8,128)S(1)} %get-tuple-element.10), channel_id=1, source_target_pairs={{0,1},{1,2},{2,3},{3,4},{4,5},{5,6},{6,7},{7,8},{8,9},{9,10},{10,1... | collective-permute-start | bytes 294920 | tf_op jit(solution)/shard_map/ppermute | solution.py:17
  22.4 8.0 %collective-permute-start.1 = (f32[3,64,128]{2,1,0:T(8,128)S(1)}, f32[3,64,128]{2,1,0:T(8,128)S(1)}, u32[]{:S(2)}, u32[]{:S(2)}) collective-permute-start(f32[3,64,128]{2,1,0:T(8,128)S(1)} %get-tuple-element.11), channel_id=1, source_target_pairs={{1,0},{2,1},{3,2},{4,3},{5,4},{6,5},{7,6},{8,7},{9,8},{10,9},{11,1... | collective-permute-start | bytes 294920 | tf_op jit(solution)/shard_map/ppermute | solution.py:18
  37.8 1.0 copy-start.3
  37.9 2.9 collective-permute-start.2
  46.6 238.0 %all-gather.9.cloned.1.call-start = ((), (), s32[]{:S(2)}) async-start(), calls=%async_computation.2 | async-start | bytes 8650752 | tf_op jit(solution)/shard_map/all_gather | solution.py:45
  160.8 24.5 %collective-permute-start.3 = (f32[2048,128]{0,1:T(8,128)}, f32[2048,128]{0,1:T(8,128)}, u32[]{:S(2)}, u32[]{:S(2)}) collective-permute-start(f32[2048,128]{0,1:T(8,128)} %fusion.9), channel_id=1, source_target_pairs={{0,64},{64,0},{32,96},{96,32},{128,192},{192,128},{160,224},{224,1... | collective-permute-start | bytes 3145736 | tf_op jit(solution)/shard_map/ppermute | solution.py:30
  189.6 236.2 %all-gather.11.cloned.1.call-start = ((), (), s32[]{:S(2)}) async-start(), calls=%async_computation.3 | async-start | bytes 8650752 | tf_op jit(solution)/shard_map/all_gather | solution.py:45
  299.8 25.9 %collective-permute-start.4 = (f32[2048,128]{0,1:T(8,128)}, f32[2048,128]{0,1:T(8,128)S(1)}, u32[]{:S(2)}, u32[]{:S(2)}) collective-permute-start(f32[2048,128]{0,1:T(8,128)} %fusion.7), channel_id=1, source_target_pairs={{0,128},{128,0},{32,160},{160,32},{64,192},{192,64},{96,224},{224,... | collective-permute-start | bytes 3145736 | tf_op jit(solution)/shard_map/ppermute | solution.py:30
  327.0 1.1 copy-start.1
  330.7 250.9 %all-reduce.2.cloned.1.call-start = ((), (), s32[]{:S(2)}) async-start(), calls=%async_computation | async-start | bytes 131072 | tf_op jit(solution)/shard_map/psum | solution.py:87
  436.7 2.0 copy-start.2
Sparse Core Ops, SparseCore 0:
  46.7 97.8 all-gather.6
  189.7 94.8 all-gather.8
  330.8 94.8 all-gather.10
  441.9 139.6 all-reduce.1
